TPU v7x, 256 devices: a whole 4x4x8 slice. The times are simulated.
256 devices in a mesh: tok: 128 (over x, y, z_lo, core), mem: 2 (over z_hi).
Axes of the slice: x: 4, y: 4, z: 8 (z_hi: 2, z_lo: 4; z = z_hi * 4 + z_lo), core: 2. Of those that a mesh axis runs over, the one named last changes fastest.
Arguments:
- queries: bfloat16 [65536, 1024], P('tok', 'mem'), may hold values from -6 to 6
- keys: bfloat16 [65536, 1024], P('tok', 'mem'), may hold values from -6 to 6
- values: bfloat16 [65536, 1024], P('tok', 'mem'), may hold values from -6 to 6
- step_sizes: float32 [4, 65536], P(None, 'tok'), may hold values from 0.05 to 0.5
- fast_weights: float32 [4, 256, 768], P(None, 'mem'), may hold values from -0.375 to 0.375
- view_lengths: int32 [256], replicated, may hold values from 1 to 512, 65536 in all
Outputs:
- layer_out: bfloat16 [65536, 1024], P('tok', 'mem')
Inputs may be any that keep to these rules, and one draw needn't show every extreme that they name: `view_lengths`: the lengths sum to 65536 and the longest view has exactly 512 tokens.
All inputs are finite; a program needn't handle non-finite values.
Results may differ from a plain program's by a relative error of at most 0.011.
Values may be sent and summed in bfloat16 or wider, within the bound.
A program may use at most 64 MiB of HBM per device.

v0:
```python
import math

import jax
import jax.numpy as jnp
from jax import lax
from jax.sharding import PartitionSpec as P

DM = 256
HD = 128


norm_epsilon = 1e-06


def extended(cells, sides, width):
    for axis, dim in sides:
        count = lax.axis_size(axis)
        ends = count - 1
        head = lax.slice_in_dim(cells, 0, width, axis=dim)
        tail = lax.slice_in_dim(cells, cells.shape[dim] - width, cells.shape[dim], axis=dim)
        cells = jnp.concatenate(
            [
                lax.ppermute(tail, axis, [(i, (i + 1) % count) for i in range(ends)]),
                cells,
                lax.ppermute(head, axis, [((i + 1) % count, i) for i in range(ends)]),
            ],
            axis=dim,
        )
    return cells


def silu_pair(pre_act):
    sigmoid_val = jax.nn.sigmoid(pre_act)
    return (pre_act * sigmoid_val, sigmoid_val * (1.0 + pre_act * (1.0 - sigmoid_val)))


def attend(queries, beside_all, same_view):
    tok_rows = queries.shape[0]
    feat_width = queries.shape[1]
    head_count = feat_width // HD
    score_scale = 1.0 / math.sqrt(HD)

    def one_head(head_index, result):
        offset = head_index * HD
        query_head = lax.dynamic_slice_in_dim(queries, offset, HD, 1)
        key_head = lax.dynamic_slice_in_dim(beside_all[0], offset, HD, 1)
        value_head = lax.dynamic_slice_in_dim(beside_all[1], offset, HD, 1)
        scores = (
            jnp.einsum("qd,kd->qk", query_head, key_head, preferred_element_type=jnp.float32)
            * score_scale
        )
        scores = jnp.where(same_view, scores, -1e30)
        row_peak = jnp.max(scores, axis=1, keepdims=True)
        exponent = jnp.exp(scores - row_peak)
        probs = (exponent / jnp.sum(exponent, axis=1, keepdims=True)).astype(jnp.bfloat16)
        output = jnp.dot(probs, value_head, preferred_element_type=jnp.float32)
        return lax.dynamic_update_slice_in_dim(result, output, offset, 1)

    return lax.fori_loop(0, head_count, one_head, jnp.zeros((tok_rows, feat_width), jnp.float32))


def memory_grads(key_part, value_part, token_rates, weights):
    rounded = weights.astype(jnp.bfloat16)
    weight_in = rounded[:, :DM]
    weight_up = rounded[:, DM : 2 * DM]
    weight_out = rounded[:, 2 * DM :]
    gate_pre = jnp.einsum("td,fd->tf", key_part, weight_in, preferred_element_type=jnp.float32)
    up_pre = jnp.einsum("td,fd->tf", key_part, weight_up, preferred_element_type=jnp.float32)
    swish_val, slope_val = silu_pair(gate_pre)
    hidden = (swish_val * up_pre).astype(jnp.bfloat16)
    scaled = (token_rates[:, None] * value_part.astype(jnp.float32)).astype(jnp.bfloat16)
    grad_out = -jnp.einsum("tf,td->fd", hidden, scaled, preferred_element_type=jnp.float32)
    back_flow = -jnp.einsum("td,fd->tf", scaled, weight_out, preferred_element_type=jnp.float32)
    gate_back = (back_flow * up_pre * slope_val).astype(jnp.bfloat16)
    up_back = (back_flow * swish_val).astype(jnp.bfloat16)
    grad_in = jnp.einsum("tf,td->fd", gate_back, key_part, preferred_element_type=jnp.float32)
    grad_up = jnp.einsum("tf,td->fd", up_back, key_part, preferred_element_type=jnp.float32)
    return jnp.concatenate([grad_in, grad_up, grad_out], axis=1)


def memory_read(query_part, weights):
    rounded = weights.astype(jnp.bfloat16)
    gate_pre = jnp.einsum(
        "td,fd->tf", query_part, rounded[:, :DM], preferred_element_type=jnp.float32
    )
    up_pre = jnp.einsum(
        "td,fd->tf", query_part, rounded[:, DM : 2 * DM], preferred_element_type=jnp.float32
    )
    swish_val, slope_val = silu_pair(gate_pre)
    read_hidden = (swish_val * up_pre).astype(jnp.bfloat16)
    return jnp.dot(read_hidden, rounded[:, 2 * DM :], preferred_element_type=jnp.float32)


def renormed(weights, gradient, step_rate):
    stepped = weights - gradient * step_rate
    shaped = stepped.reshape(stepped.shape[0], 3, DM)
    before = weights.reshape(weights.shape[0], 3, DM)
    old_norm = jnp.sqrt(jnp.sum(before * before, axis=2))
    new_norm = jnp.sqrt(jnp.sum(shaped * shaped, axis=2) + norm_epsilon)
    return (shaped * (old_norm / new_norm)[:, :, None]).reshape(stepped.shape)


def reduce_update(gradient, weights, step_rate):
    unit_count = gradient.shape[0] * gradient.shape[1]
    flat_grad = gradient.reshape(unit_count, 3 * DM)
    flat_weight = weights.reshape(unit_count, 3 * DM)
    summed = lax.psum(flat_grad, "tok")
    updated = renormed(flat_weight, summed, step_rate)
    return updated.reshape(weights.shape)


def on_device(queries, keys, values, step_sizes, fast_weights, view_lengths):
    tok_rows = queries.shape[0]
    all_tokens = tok_rows * lax.axis_size("tok")
    stacked = jnp.stack([keys, values])
    beside_all = extended(stacked, (("tok", 1),), tok_rows)
    view_ends = jnp.cumsum(view_lengths)
    row_start = lax.axis_index("tok") * tok_rows
    key_spots = row_start - tok_rows + jnp.arange(3 * tok_rows, dtype=jnp.int32)
    key_views = jnp.sum((view_ends[None, :] <= key_spots[:, None]).astype(jnp.int32), axis=1)
    key_views = jnp.where((key_spots >= 0) & (key_spots < all_tokens), key_views, -1)
    query_views = key_views[tok_rows : 2 * tok_rows]
    same_view = query_views[:, None] == key_views[None, :]
    attended = attend(queries, beside_all, same_view)
    step_rate = 1.0 / math.sqrt(all_tokens)
    features = (
        lax.all_gather(queries, "mem", axis=1, tiled=True),
        lax.all_gather(keys, "mem", axis=1, tiled=True),
        lax.all_gather(values, "mem", axis=1, tiled=True),
    )
    gradient = jnp.stack(
        [
            memory_grads(
                features[1][:, memory * DM : (memory + 1) * DM],
                features[2][:, memory * DM : (memory + 1) * DM],
                step_sizes[memory],
                fast_weights[memory],
            )
            for memory in range(fast_weights.shape[0])
        ]
    )
    updated = reduce_update(gradient, fast_weights, step_rate)
    memory_out = jnp.concatenate(
        [
            memory_read(features[0][:, memory * DM : (memory + 1) * DM], updated[memory])
            for memory in range(fast_weights.shape[0])
        ],
        axis=1,
    )
    memory_out = lax.psum_scatter(memory_out, "mem", scatter_dimension=1, tiled=True)
    return (attended + memory_out).astype(jnp.bfloat16)


def solution(mesh):
    placed = (
        P("tok", "mem"),
        P("tok", "mem"),
        P("tok", "mem"),
        P(None, "tok"),
        P(None, "mem", None),
        P(),
    )
    return jax.shard_map(
        on_device, mesh=mesh, in_specs=placed, out_specs=P("tok", "mem"), check_vma=False
    )
```

profile of v0, /device:TPU:1, one launch (start us, length us, event | category | flops | bytes accessed | tf_op | source)
XLA Modules:
  0.0 1503.5 jit_solution(4722010981132420041)
XLA Ops:
  8.9 2.2 fusion.151
  11.1 43.5 %all-gather.6.cloned.1.call-done = bf16[512,1024]{1,0:T(8,128)(2,1)} async-done(((bf16[512,512]{1,0:T(8,128)(2,1)}), bf16[512,1024]{1,0:T(8,128)(2,1)}) %all-gather.6.cloned.1.call-update) | async-done | bytes 1048592 | tf_op jit(solution)/shard_map/all_gather | solution.py:128
  54.7 2.0 fusion.75
  56.7 1.9 fusion.73
  58.6 36.2 %all-gather.4.cloned.1.call-done = bf16[512,1024]{1,0:T(8,128)(2,1)} async-done(((bf16[512,512]{1,0:T(8,128)(2,1)}), bf16[512,1024]{1,0:T(8,128)(2,1)}) %all-gather.4.cloned.1.call-update) | async-done | bytes 1048592 | tf_op jit(solution)/shard_map/all_gather | solution.py:129
  105.3 2.4 pad_maximum_fusion.3
  107.7 2.7 collective-permute-start.1
  110.4 2.8 collective-permute-start
  117.8 18.5 %collective-permute-done.1 = bf16[2,512,512]{2,1,0:T(8,128)(2,1)} collective-permute-done((bf16[2,512,512]{2,1,0:T(8,128)(2,1)}, bf16[2,512,512]{2,1,0:T(8,128)(2,1)}, u32[]{:S(2)}, u32[]{:S(2)}) %collective-permute-start.1) | collective-permute-done | bytes 1048608 | tf_op jit(solution)/shard_map/ppermute | solution.py:25
  136.3 2.0 pad_maximum_fusion
  138.3 1233.2 %all-reduce.2.cloned.1.call-done = f32[512,768]{0,1:T(8,128)} async-done(((f32[512,768]{0,1:T(8,128)}), f32[512,768]{0,1:T(8,128)}) %all-reduce.2.cloned.1.call-update) | async-done | bytes 1572880 | tf_op jit(solution)/shard_map/psum | solution.py:107
  1371.6 2.2 multiply_subtract_fusion
  1375.1 39.0 %all-gather.8.cloned.1.call-done = bf16[512,1024]{1,0:T(8,128)(2,1)} async-done(((bf16[512,512]{1,0:T(8,128)(2,1)}), bf16[512,1024]{1,0:T(8,128)(2,1)}) %all-gather.8.cloned.1.call-update) | async-done | bytes 1048592 | tf_op jit(solution)/shard_map/all_gather | solution.py:127
  1414.1 1.9 convolution_bitcast_fusion.1
  1416.0 2.3 fusion.21
  1418.3 1.9 convolution_bitcast_fusion.3
  1420.2 2.3 fusion.22
  1422.5 1.9 convolution_bitcast_fusion.5
  1424.4 2.3 fusion.23
  1426.7 1.9 convolution_bitcast_fusion.7
  1428.5 2.3 fusion.24
  1430.8 3.0 pad_maximum_fusion.1
  1435.0 16.2 %while.14 = (s32[]{:T(128)}, f32[512,512]{0,1:T(8,128)}, bf16[512,512]{1,0:T(8,128)(2,1)}, bf16[2,1536,512]{2,1,0:T(8,128)(2,1)S(1)}, s32[1536]{0:T(1024)S(1)}, ...) while((s32[]{:T(128)}, f32[512,512]{0,1:T(8,128)}, ...), condition=%wide.region_6.7_spmd.clone, body=%wide.region_3.6_spmd.clone.sunk | while | flops 409730048 | bytes 16930972 | solution.py:59
  1451.2 43.1 %reduce-scatter.2.cloned.1.call-done = f32[512,512]{0,1:T(8,128)} async-done(((f32[512,1024]{0,1:T(8,128)}), f32[512,512]{0,1:T(8,128)}) %reduce-scatter.2.cloned.1.call-update) | async-done | bytes 1048592 | tf_op jit(solution)/shard_map/reduce_scatter | solution.py:150
  (87 shorter events, 38.5 us)
Async XLA Ops:
  6.5 48.2 %all-gather.6.cloned.1.call-start = ((), (), s32[]{:S(2)}) async-start(), calls=%async_computation.2 | async-start | bytes 1572864 | tf_op jit(solution)/shard_map/all_gather | solution.py:128
  7.3 87.5 %all-gather.4.cloned.1.call-start = ((), (), s32[]{:S(2)}) async-start(), calls=%async_computation.1 | async-start | bytes 1572864 | tf_op jit(solution)/shard_map/all_gather | solution.py:129
  8.0 1363.5 %all-reduce.2.cloned.1.call-start = ((), (), s32[]{:S(2)}) async-start(), calls=%async_computation.3 | async-start | bytes 3145728 | tf_op jit(solution)/shard_map/psum | solution.py:107
  54.7 42.8 %copy-start.1 = (bf16[512,1024]{1,0:T(8,128)(2,1)S(1)}, bf16[512,1024]{1,0:T(8,128)(2,1)}, u32[]{:S(2)}) copy-start(bf16[512,1024]{1,0:T(8,128)(2,1)} %all-gather.6.cloned.1.call-done) | copy-start | bytes 3145732
  94.8 2.7 copy-start.3
  94.8 3.0 copy-start.2
  97.5 1.2 copy-start.5
  105.2 8.3 copy-start.4
  105.2 9.5 copy-start
  105.2 1308.9 %all-gather.8.cloned.1.call-start = ((), (), s32[]{:S(2)}) async-start(), calls=%async_computation.4 | async-start | bytes 1572864 | tf_op jit(solution)/shard_map/all_gather | solution.py:127
  107.7 28.6 %collective-permute-start.1 = (bf16[2,512,512]{2,1,0:T(8,128)(2,1)}, bf16[2,512,512]{2,1,0:T(8,128)(2,1)}, u32[]{:S(2)}, u32[]{:S(2)}) collective-permute-start(bf16[2,512,512]{2,1,0:T(8,128)(2,1)} %pad_maximum_fusion.3), channel_id=1, source_target_pairs={{2,0},{4,2},{6,4},{8,6},{10,8},{12,10},{14,12},{16,14},{18,16},{20... | collective-permute-start | bytes 3145736 | tf_op jit(solution)/shard_map/ppermute | solution.py:25
  110.4 25.9 %collective-permute-start = (bf16[2,512,512]{2,1,0:T(8,128)(2,1)}, bf16[2,512,512]{2,1,0:T(8,128)(2,1)}, u32[]{:S(2)}, u32[]{:S(2)}) collective-permute-start(bf16[2,512,512]{2,1,0:T(8,128)(2,1)} %pad_maximum_fusion.3), channel_id=1, source_target_pairs={{0,2},{2,4},{4,6},{6,8},{8,10},{10,12},{12,14},{14,16},{16,18},{18... | collective-permute-start | bytes 3145736 | tf_op jit(solution)/shard_map/ppermute | solution.py:23
  113.3 1381.0 %reduce-scatter.2.cloned.1.call-start = ((), (), s32[]{:S(2)}) async-start(), calls=%async_computation.5 | async-start | bytes 3145728 | tf_op jit(solution)/shard_map/reduce_scatter | solution.py:150
Sparse Core Ops, SparseCore 0:
  9.1 45.5 all-gather.5
  56.5 38.2 all-gather.3
  105.3 1266.1 all-reduce.1
  1373.2 40.8 all-gather.7
  1434.0 60.2 reduce-scatter.1
where the time goes:
time: 1500 us
  waiting for transfers between devices  1410 us (94%)
  matrix products  41.9 us (3%)
  other arithmetic  17.5 us (1%)
    psum x1, waiting for transfers between devices, reduce_update(): summed = lax.psum(flat_grad, 'tok')  1230 us
    all_gather x1, waiting for transfers between devices, on_device(): lax.all_gather(keys, 'mem', axis=1, tiled=True)  43.5 us
    reduce_scatter x1, waiting for transfers between devices, on_device(): lax.psum_scatter(memory_out, 'mem', scatter_dimension=1, tiled=True)  43.1 us
    all_gather x1, waiting for transfers between devices, on_device(): lax.all_gather(queries, 'mem', axis=1, tiled=True)  39 us
    all_gather x1, waiting for transfers between devices, on_device(): lax.all_gather(values, 'mem', axis=1, tiled=True)  36.2 us
  transfers between devices with their start and end apart: 7, of which 6 were waited for; matrix products, arithmetic and copies ran while one was open for 2% of the time, Pallas kernels for 0%

commit v1 on v0

v1 whole, which is shorter than its diff:
```python
import math

import jax
import jax.numpy as jnp
from jax import lax
from jax.experimental import pallas as pl
from jax.experimental.pallas import tpu as pltpu
from jax.sharding import PartitionSpec as P

DM = 256
HD = 128
PLANE = 16
COLUMN = 4
UNITS = 128
PIECE = UNITS // PLANE
WIDE = 3 * DM
MESH = pl.DeviceIdType.MESH
NT = (((1,), (1,)), ((), ()))
NN = (((1,), (0,)), ((), ()))

norm_epsilon = 1e-06


def dot(a, b, dims):
    return lax.dot_general(a, b, dims, preferred_element_type=jnp.float32)


def flat(pieces):
    return pieces.astype(jnp.float32).reshape(UNITS, WIDE)


def body(
    q_ref, k_ref, v_ref, step_ref, fw_ref, len_ref, out_ref,
    kx, vx, acc, kid, qid,
    cross, wo, part, inbox, piece_out, piece_in, col_out, col_in, nw,
    sems, half_sems, halo_sems,
):
    tok = lax.axis_index("tok")
    mem = lax.axis_index("mem")
    n_tok = lax.axis_size("tok")
    rows = q_ref.shape[0]
    core = lax.rem(tok, 2)
    other = 1 - core
    plane = tok // 8
    spot = lax.rem(tok, 8)
    level = spot // 2
    partner = tok + 1 - 2 * core
    right = lax.rem(tok + 1, n_tok)
    left = lax.rem(tok + n_tok - 1, n_tok)
    total_rows = n_tok * rows
    rate = 1.0 / math.sqrt(total_rows)

    def plane_peer(d):
        return lax.rem(plane + d, PLANE) * 8 + spot

    def column_peer(d):
        return plane * 8 + lax.rem(level + d, COLUMN) * 2 + core

    def send(src, dst, s_sem, r_sem, tok_id, mem_id=None):
        return pltpu.make_async_remote_copy(
            src_ref=src, dst_ref=dst, send_sem=s_sem, recv_sem=r_sem,
            device_id={"tok": tok_id, "mem": mem if mem_id is None else mem_id},
            device_id_type=MESH,
        )

    own_k = pltpu.make_async_copy(k_ref, kx.at[pl.ds(rows, rows)], sems.at[0])
    own_v = pltpu.make_async_copy(v_ref, vx.at[pl.ds(rows, rows)], sems.at[1])
    own_k.start()
    own_v.start()

    barrier = pltpu.get_barrier_semaphore()

    def greet(tok_id, mem_id):
        pl.semaphore_signal(
            barrier, inc=1, device_id={"tok": tok_id, "mem": mem_id}, device_id_type=MESH
        )

    greet(partner, mem)
    greet(tok, 1 - mem)
    greet(left, mem)
    greet(right, mem)

    @pl.loop(1, PLANE)
    def _(d):
        greet(plane_peer(d), mem)

    @pl.loop(1, COLUMN)
    def _(d):
        greet(column_peer(d), mem)

    own_k.wait()
    own_v.wait()

    def grads(j, wb):
        lanes = pl.ds(pl.multiple_of(j * DM, DM), DM)
        kj = kx[pl.ds(rows, rows), lanes]
        vj = vx[pl.ds(rows, rows), lanes]
        step = step_ref[pl.ds(2 * mem + j, 1), :]
        pre = dot(jnp.concatenate([wb[:, :DM], wb[:, DM : 2 * DM]], axis=0), kj, NT)
        gate, up = pre[:UNITS], pre[UNITS:]
        back = -dot(wb[:, 2 * DM :], vj, NT) * step
        sig = jax.nn.sigmoid(gate)
        swish = gate * sig
        slope = sig * (1.0 + gate * (1.0 - sig))
        hidden = (swish * up * step).astype(jnp.bfloat16)
        gate_back = (back * up * slope).astype(jnp.bfloat16)
        up_back = (back * swish).astype(jnp.bfloat16)
        both = dot(jnp.concatenate([gate_back, up_back], axis=0), kj, NN)
        out = -dot(hidden, vj, NN)
        return jnp.concatenate([both[:UNITS], both[UNITS:], out], axis=1).reshape(
            PLANE, PIECE, WIDE
        )

    def core_start(half, value):
        part[half, 0] = value.astype(jnp.bfloat16)
        copy = send(part.at[half, 0], inbox.at[half], half_sems.at[half, 0], half_sems.at[half, 1], partner)
        copy.start()
        return copy

    def scatter_start(half, copy, own):
        copy.wait_recv()
        total = own[...] + inbox[half].astype(jnp.float32)
        own[...] = total
        part[half, 1] = total.astype(jnp.bfloat16)

        @pl.loop(1, PLANE)
        def _(d):
            to = lax.rem(plane + d, PLANE)
            send(
                part.at[half, 1, to], piece_in.at[half, d - 1],
                half_sems.at[half, 2], half_sems.at[half, 3], to * 8 + spot,
            ).start()

    def whole(half):
        return send(
            part.at[half, 1, pl.ds(0, PLANE - 1)], piece_in.at[half],
            half_sems.at[half, 2], half_sems.at[half, 3], plane_peer(1),
        )

    def column_start(half, own):
        whole(half).wait_recv()
        total = own[plane]
        for d in range(PLANE - 1):
            total = total + piece_in[half, d].astype(jnp.float32)
        col_out[half] = total

        @pl.loop(1, COLUMN)
        def _(d):
            send(
                col_out.at[half], col_in.at[half, d - 1],
                half_sems.at[half, 4], half_sems.at[half, 5], column_peer(d),
            ).start()

    def column_whole(half):
        return send(
            col_in.at[half], col_in.at[half],
            half_sems.at[half, 4], half_sems.at[half, 5], column_peer(1),
        )

    def update(half, before):
        column_whole(half).wait_recv()
        total = col_out[half]
        for d in range(COLUMN - 1):
            total = total + col_in[half, d]
        stepped = before - total * rate
        blocks = []
        for b in range(3):
            old = before[:, b * DM : (b + 1) * DM]
            new = stepped[:, b * DM : (b + 1) * DM]
            old_norm = jnp.sqrt(jnp.sum(old * old, axis=1, keepdims=True))
            new_norm = jnp.sqrt(jnp.sum(new * new, axis=1, keepdims=True) + norm_epsilon)
            blocks.append(new * (old_norm / new_norm))
        nw[half, core, plane] = jnp.concatenate(blocks, axis=1).astype(jnp.bfloat16)

        @pl.loop(1, PLANE)
        def _(d):
            send(
                nw.at[half, core, plane], nw.at[half, core, plane],
                half_sems.at[half, 6], half_sems.at[half, 7], plane_peer(d),
            ).start()

    def gather_whole(half):
        return send(
            nw.at[half, core, pl.ds(0, PLANE - 1)], nw.at[half, core, pl.ds(0, PLANE - 1)],
            half_sems.at[half, 6], half_sems.at[half, 7], plane_peer(1),
        )

    def swap_start(half):
        gather_whole(half).wait_recv()
        copy = send(
            nw.at[half, core], nw.at[half, core],
            half_sems.at[half, 8], half_sems.at[half, 9], partner,
        )
        copy.start()
        return copy

    own_l, own_o = piece_out.at[0], piece_out.at[1]

    away = grads(other, fw_ref[2 * mem + other].astype(jnp.bfloat16))
    own_l[...] = grads(core, fw_ref[2 * mem + core].astype(jnp.bfloat16))

    pl.semaphore_wait(barrier, PLANE - 1 + COLUMN - 1 + 4)

    first = pl.ds(pl.multiple_of(plane * PIECE, PIECE), PIECE)
    crossing = send(
        fw_ref.at[2 * (1 - mem) + core, first], cross,
        sems.at[2], sems.at[3], tok, 1 - mem,
    )
    crossing.start()
    core_l = core_start(0, away)

    halos = []
    middle = pl.ds(rows, rows)
    for n, buf in enumerate((kx, vx)):
        halos.append(send(buf.at[middle], buf.at[pl.ds(0, rows)], halo_sems.at[n, 0], halo_sems.at[n, 1], right))
        halos.append(send(buf.at[middle], buf.at[pl.ds(2 * rows, rows)], halo_sems.at[n, 2], halo_sems.at[n, 3], left))
    for copy in halos:
        copy.start()

    scatter_start(0, core_l, own_l)

    crossing.wait_recv()
    wo[core, plane] = cross[...].astype(jnp.bfloat16)

    @pl.loop(1, PLANE)
    def _(d):
        send(
            wo.at[core, plane], wo.at[core, plane], sems.at[4], sems.at[5], plane_peer(d)
        ).start()

    count = len_ref.shape[1]
    lengths = len_ref[...].astype(jnp.float32)
    square = (count, count)
    down = lax.broadcasted_iota(jnp.int32, square, 0)
    along = lax.broadcasted_iota(jnp.int32, square, 1)
    spread = jnp.broadcast_to(lengths, square)
    ends_col = jnp.sum(jnp.where(along <= down, spread, 0.0), axis=1, keepdims=True)
    len_col = jnp.sum(jnp.where(along == down, spread, 0.0), axis=1, keepdims=True)
    ends_row = jnp.sum(jnp.where(down <= along, len_col, 0.0), axis=0, keepdims=True)
    base = tok * rows
    spots = base - rows + lax.broadcasted_iota(jnp.int32, (1, 3 * rows), 1)
    spots_f = spots.astype(jnp.float32)
    key_views = jnp.sum(jnp.where(ends_col <= spots_f, 1.0, 0.0), axis=0, keepdims=True)
    kid[...] = jnp.where((spots >= 0) & (spots < total_rows), key_views, -1.0)
    rows_f = (base + lax.broadcasted_iota(jnp.int32, (rows, 1), 0)).astype(jnp.float32)
    query_views = jnp.sum(jnp.where(ends_row <= rows_f, 1.0, 0.0), axis=1, keepdims=True)
    qid[...] = jnp.broadcast_to(query_views, (rows, HD))

    gathered = send(
        wo.at[core, pl.ds(0, PLANE - 1)], wo.at[core, pl.ds(0, PLANE - 1)],
        sems.at[4], sems.at[5], plane_peer(1),
    )
    gathered.wait_recv()
    swapped = send(wo.at[core], wo.at[core], sems.at[6], sems.at[7], partner)
    swapped.start()

    own_o[...] = grads(core, flat(wo[core]).astype(jnp.bfloat16))
    swapped.wait_recv()
    core_o = core_start(1, grads(other, flat(wo[other]).astype(jnp.bfloat16)))

    column_start(0, own_l)
    scatter_start(1, core_o, own_o)
    update(0, fw_ref[2 * mem + core, first])
    column_start(1, own_o)
    swap_l = swap_start(0)
    update(1, cross[...])

    for copy in halos:
        copy.wait_recv()

    factor = 1.0 / math.sqrt(HD) * math.log2(math.e)
    heads = q_ref.shape[1] // HD
    reach = rows + rows + HD

    @pl.loop(0, rows // HD)
    def _(i):
        here = pl.ds(pl.multiple_of(i * HD, HD), HD)
        keys = pl.ds(pl.multiple_of(i * HD, HD), reach)
        same = qid[here, :1] == kid[:, keys]
        for h in range(heads):
            lanes = slice(h * HD, (h + 1) * HD)
            scores = dot(q_ref[here, lanes], kx[keys, lanes], NT)
            scores = jnp.where(same, scores * factor, -1e30)
            peak = jnp.max(scores, axis=1, keepdims=True)
            weight = jnp.exp2(scores - peak)
            mass = jnp.sum(weight, axis=1, keepdims=True)
            acc[here, lanes] = dot(weight.astype(jnp.bfloat16), vx[keys, lanes], NN) / mass

    swap_l.wait_recv()
    swap_o = swap_start(1)

    def read(half, j):
        w = flat(nw[half, j]).astype(jnp.bfloat16)
        qj = q_ref[:, j * DM : (j + 1) * DM]
        pre = dot(qj, jnp.concatenate([w[:, :DM], w[:, DM : 2 * DM]], axis=0), NT)
        gate, up = pre[:, :UNITS], pre[:, UNITS:]
        hidden = (gate * jax.nn.sigmoid(gate) * up).astype(jnp.bfloat16)
        return dot(hidden, w[:, 2 * DM :], NN)

    for j in range(2):
        lanes = slice(j * DM, (j + 1) * DM)
        acc[:, lanes] = acc[:, lanes] + read(0, j)
    swap_o.wait_recv()
    for j in range(2):
        lanes = slice(j * DM, (j + 1) * DM)
        out_ref[:, lanes] = (acc[:, lanes] + read(1, j)).astype(jnp.bfloat16)

    crossing.wait_send()
    gathered.wait_send()
    swapped.wait_send()
    for copy in halos:
        copy.wait_send()
    for half, (first_copy, last_copy) in enumerate(((core_l, swap_l), (core_o, swap_o))):
        first_copy.wait_send()
        whole(half).wait_send()
        column_whole(half).wait_send()
        gather_whole(half).wait_send()
        last_copy.wait_send()


def on_device(queries, keys, values, step_sizes, fast_weights, view_lengths):
    rows, feats = queries.shape
    vmem = pl.BlockSpec(memory_space=pltpu.VMEM)
    hbm = pl.BlockSpec(memory_space=pl.ANY)
    bf, f32 = jnp.bfloat16, jnp.float32
    pieces = (PLANE, PIECE, WIDE)
    return pl.pallas_call(
        body,
        out_shape=jax.ShapeDtypeStruct((rows, feats), bf),
        in_specs=[vmem, hbm, hbm, vmem, vmem, vmem],
        out_specs=vmem,
        scratch_shapes=[
            pltpu.VMEM((3 * rows, feats), bf),
            pltpu.VMEM((3 * rows, feats), bf),
            pltpu.VMEM((rows, feats), f32),
            pltpu.VMEM((1, 3 * rows), f32),
            pltpu.VMEM((rows, HD), f32),
            pltpu.VMEM((PIECE, WIDE), f32),
            pltpu.VMEM((2,) + pieces, bf),
            pltpu.VMEM((2, 2) + pieces, bf),
            pltpu.VMEM((2,) + pieces, bf),
            pltpu.VMEM((2,) + pieces, f32),
            pltpu.VMEM((2, PLANE - 1, PIECE, WIDE), bf),
            pltpu.VMEM((2, PIECE, WIDE), f32),
            pltpu.VMEM((2, COLUMN - 1, PIECE, WIDE), f32),
            pltpu.VMEM((2, 2) + pieces, bf),
            pltpu.SemaphoreType.DMA((8,)),
            pltpu.SemaphoreType.DMA((2, 10)),
            pltpu.SemaphoreType.DMA((2, 4)),
        ],
        compiler_params=pltpu.CompilerParams(
            collective_id=0, has_side_effects=True, vmem_limit_bytes=48 * 1024 * 1024
        ),
    )(queries, keys, values, step_sizes, fast_weights, view_lengths.reshape(1, -1))


def solution(mesh):
    placed = (
        P("tok", "mem"),
        P("tok", "mem"),
        P("tok", "mem"),
        P(None, "tok"),
        P(None, "mem", None),
        P(),
    )
    return jax.shard_map(
        on_device, mesh=mesh, in_specs=placed, out_specs=P("tok", "mem"), check_vma=False
    )
```

time: 1500 us -> 60.5 us (0.04)
  waiting for transfers between devices: 1410 us -> 0 us
  Pallas kernels: 0 us -> 53.5 us
  matrix products: 41.9 us -> 0 us
  other arithmetic: 17.5 us -> 0 us
    psum x1 -> x0, waiting for transfers between devices: 1230 us -> none  [reduce_update(): summed = lax.psum(flat_grad, 'tok')]
    all_gather x3 -> x0, waiting for transfers between devices: 119 us -> none  [the longest x1 43.5 us: on_device(): lax.all_gather(keys, 'mem', axis=1, tiled=True)]
    pallas_call x0 -> x1, Pallas kernels: none -> 53.5 us  [on_device(): pl.pallas_call(body, out_shape=jax.ShapeDtypeStruct((rows, feats), bf), i...]
    reduce_scatter x1 -> x0, waiting for transfers between devices: 43.1 us -> none  [on_device(): lax.psum_scatter(memory_out, 'mem', scatter_dimension=1, tiled=True)]
    dot_general x36 -> x0, matrix products: 35.4 us -> none  [the longest x4 9.26 us: memory_read(): jnp.dot(read_hidden, rounded[:, 2 * DM:], preferred_element_type=jnp.floa...]
    ppermute x2 -> x0, waiting for transfers between devices: 18.5 us -> none  [the longest x1 18.5 us: extended(): lax.ppermute(head, axis, [((i + 1) % count, i) for i in range(ends)])]
  transfers between devices with their start and end apart: 7 -> 0, of which waited for: 6 -> 0; matrix products, arithmetic and copies ran while one was open for 2% -> 0% of each run, Pallas kernels for 0% -> 0%
where the time goes in v1:
time: 60.5 us; the launch traced here: 60.2 us
  Pallas kernels  53.5 us (88%)
  local copies, waits for them, and re-layouts  6.7 us (11%)
    pallas_call x1, Pallas kernels, on_device(): pl.pallas_call(body, out_shape=jax.ShapeDtypeStruct((rows, feats), bf), i...  53.5 us
    unnamed x13, local copies, waits for them, and re-layouts  6.7 us

profile of v1, /device:TPU:1, one launch (start us, length us, event | category | flops | bytes accessed | tf_op | source)
XLA Modules:
  0.0 60.2 jit_solution(16072057822434175401)
XLA Ops:
  0.0 0.0 copy-start
  0.0 1.4 %copy-done = f32[4,128,768]{2,1,0:T(8,128)S(1)} copy-done((f32[4,128,768]{2,1,0:T(8,128)S(1)}, f32[4,128,768]{2,1,0:T(8,128)}, u32[]{:S(2)}) %copy-start) | copy-done | bytes 1572888
  1.4 0.0 copy-start.1
  1.4 1.0 %copy-done.1 = bf16[512,512]{1,0:T(8,128)(2,1)S(1)} copy-done((bf16[512,512]{1,0:T(8,128)(2,1)S(1)}, bf16[512,512]{1,0:T(8,128)(2,1)}, u32[]{:S(2)}) %copy-start.1) | copy-done | bytes 524312
  2.5 0.0 copy-start.2
  2.5 1.0 %copy-done.2 = bf16[512,512]{1,0:T(8,128)(2,1)S(1)} copy-done((bf16[512,512]{1,0:T(8,128)(2,1)S(1)}, bf16[512,512]{1,0:T(8,128)(2,1)}, u32[]{:S(2)}) %copy-start.2) | copy-done | bytes 524312
  3.5 0.0 copy-start.3
  3.5 1.0 %copy-done.3 = bf16[512,512]{1,0:T(8,128)(2,1)S(1)} copy-done((bf16[512,512]{1,0:T(8,128)(2,1)S(1)}, bf16[512,512]{1,0:T(8,128)(2,1)}, u32[]{:S(2)}) %copy-start.3) | copy-done | bytes 524312
  4.5 0.0 copy-start.4
  4.5 0.7 %copy-done.4 = f32[4,512]{1,0:T(4,128)S(1)} copy-done((f32[4,512]{1,0:T(4,128)S(1)}, f32[4,512]{1,0:T(4,128)}, u32[]{:S(2)}) %copy-start.4) | copy-done | bytes 8216
  5.2 0.0 copy-start.5
  5.2 0.7 %copy-done.5 = s32[256]{0:T(256)S(1)} copy-done((s32[256]{0:T(256)S(1)}, s32[256]{0:T(256)}, u32[]{:S(2)}) %copy-start.5) | copy-done | bytes 1048
  5.9 53.5 %shard_map.64 = bf16[512,512]{1,0:T(8,128)(2,1)S(1)} custom-call(bf16[512,512]{1,0:T(8,128)(2,1)S(1)} %copy-done.1, bf16[512,512]{1,0:T(8,128)(2,1)S(1)} %copy-done.2, bf16[512,512]{1,0:T(8,128)(2,1)S(1)} %copy-done.3, f32[4,512]{1,0:T(4,128)S(1)} %copy-done.4, f32[4,128,768]{2,1,0:T(8,128)S(1)} %copy-done, s32[1,256]{1,0:T(1,128)S(1)} %bitcast.1), custom_call_target="tpu_custom_call" | custom-call | tf_op jit(solution)/shard_map/pallas_call | solution.py:327
  59.4 0.8 %copy.8 = bf16[512,512]{1,0:T(8,128)(2,1)} copy(bf16[512,512]{1,0:T(8,128)(2,1)S(1)} %shard_map.64) | data formatting | bytes 1048576
Async XLA Ops:
  0.0 1.4 %copy-start = (f32[4,128,768]{2,1,0:T(8,128)S(1)}, f32[4,128,768]{2,1,0:T(8,128)}, u32[]{:S(2)}) copy-start(f32[4,128,768]{2,1,0:T(8,128)} %fw_ref.1) | copy-start | bytes 4718596
  1.4 1.0 %copy-start.1 = (bf16[512,512]{1,0:T(8,128)(2,1)S(1)}, bf16[512,512]{1,0:T(8,128)(2,1)}, u32[]{:S(2)}) copy-start(bf16[512,512]{1,0:T(8,128)(2,1)} %q_ref.1) | copy-start | bytes 1572868
  2.5 1.0 %copy-start.2 = (bf16[512,512]{1,0:T(8,128)(2,1)S(1)}, bf16[512,512]{1,0:T(8,128)(2,1)}, u32[]{:S(2)}) copy-start(bf16[512,512]{1,0:T(8,128)(2,1)} %k_ref.1) | copy-start | bytes 1572868
  3.5 1.0 %copy-start.3 = (bf16[512,512]{1,0:T(8,128)(2,1)S(1)}, bf16[512,512]{1,0:T(8,128)(2,1)}, u32[]{:S(2)}) copy-start(bf16[512,512]{1,0:T(8,128)(2,1)} %v_ref.1) | copy-start | bytes 1572868
  4.5 0.7 %copy-start.4 = (f32[4,512]{1,0:T(4,128)S(1)}, f32[4,512]{1,0:T(4,128)}, u32[]{:S(2)}) copy-start(f32[4,512]{1,0:T(4,128)} %step_ref.1) | copy-start | bytes 24580
  5.2 0.7 %copy-start.5 = (s32[256]{0:T(256)S(1)}, s32[256]{0:T(256)}, u32[]{:S(2)}) copy-start(s32[256]{0:T(256)} %param.11) | copy-start | bytes 3076

commit v2 on v1

--- a/solution.py
+++ b/solution.py
@@ -14,7 +14,13 @@
 UNITS = 128
 PIECE = UNITS // PLANE
 WIDE = 3 * DM
+VMEM_BYTES = 66_000_000
 MESH = pl.DeviceIdType.MESH
+SIDE = 4
+FAR_FIRST = sorted(
+    (d for d in range(1, PLANE)),
+    key=lambda d: -(min(d // SIDE, SIDE - d // SIDE) + min(d % SIDE, SIDE - d % SIDE)),
+)
 NT = (((1,), (1,)), ((), ()))
 NN = (((1,), (0,)), ((), ()))
 
@@ -30,15 +36,16 @@
 
 
 def body(
-    q_ref, k_ref, v_ref, step_ref, fw_ref, len_ref, out_ref,
-    kx, vx, acc, kid, qid,
+    q_hbm, k_hbm, v_hbm, step_hbm, fw_hbm, len_hbm, out_ref,
+    q_ref, step_ref, fw_ref, len_ref, kx, vx, acc, top, mass, told, kid, qid,
     cross, wo, part, inbox, piece_out, piece_in, col_out, col_in, nw,
-    sems, half_sems, halo_sems,
+    sems, half_sems, halo_sems, load_sems,
 ):
     tok = lax.axis_index("tok")
     mem = lax.axis_index("mem")
     n_tok = lax.axis_size("tok")
     rows = q_ref.shape[0]
+    mine = pl.ds(2 * mem, 2)
     core = lax.rem(tok, 2)
     other = 1 - core
     plane = tok // 8
@@ -50,8 +57,12 @@
     total_rows = n_tok * rows
     rate = 1.0 / math.sqrt(total_rows)
 
+    def plane_at(d):
+        across = lax.rem(plane // SIDE + d // SIDE, SIDE)
+        return across * SIDE + lax.rem(lax.rem(plane, SIDE) + d % SIDE, SIDE)
+
     def plane_peer(d):
-        return lax.rem(plane + d, PLANE) * 8 + spot
+        return plane_at(d) * 8 + spot
 
     def column_peer(d):
         return plane * 8 + lax.rem(level + d, COLUMN) * 2 + core
@@ -63,10 +74,20 @@
             device_id_type=MESH,
         )
 
-    own_k = pltpu.make_async_copy(k_ref, kx.at[pl.ds(rows, rows)], sems.at[0])
-    own_v = pltpu.make_async_copy(v_ref, vx.at[pl.ds(rows, rows)], sems.at[1])
-    own_k.start()
-    own_v.start()
+    middle = pl.ds(rows, rows)
+    loads = [
+        pltpu.make_async_copy(src, dst, load_sems.at[n])
+        for n, (src, dst) in enumerate((
+            (fw_hbm.at[mine], fw_ref),
+            (k_hbm, kx.at[middle]),
+            (v_hbm, vx.at[middle]),
+            (step_hbm, step_ref),
+            (len_hbm, len_ref),
+            (q_hbm, q_ref),
+        ))
+    ]
+    for load in loads:
+        load.start()
 
     barrier = pltpu.get_barrier_semaphore()
 
@@ -80,16 +101,15 @@
     greet(left, mem)
     greet(right, mem)
 
-    @pl.loop(1, PLANE)
-    def _(d):
+    for d in FAR_FIRST:
         greet(plane_peer(d), mem)
 
     @pl.loop(1, COLUMN)
     def _(d):
         greet(column_peer(d), mem)
 
-    own_k.wait()
-    own_v.wait()
+    for load in loads[:4]:
+        load.wait()
 
     def grads(j, wb):
         lanes = pl.ds(pl.multiple_of(j * DM, DM), DM)
@@ -123,9 +143,8 @@
         own[...] = total
         part[half, 1] = total.astype(jnp.bfloat16)
 
-        @pl.loop(1, PLANE)
-        def _(d):
-            to = lax.rem(plane + d, PLANE)
+        for d in FAR_FIRST:
+            to = plane_at(d)
             send(
                 part.at[half, 1, to], piece_in.at[half, d - 1],
                 half_sems.at[half, 2], half_sems.at[half, 3], to * 8 + spot,
@@ -142,7 +161,7 @@
         total = own[plane]
         for d in range(PLANE - 1):
             total = total + piece_in[half, d].astype(jnp.float32)
-        col_out[half] = total
+        col_out[half] = total.astype(jnp.bfloat16)
 
         @pl.loop(1, COLUMN)
         def _(d):
@@ -159,9 +178,9 @@
 
     def update(half, before):
         column_whole(half).wait_recv()
-        total = col_out[half]
+        total = col_out[half].astype(jnp.float32)
         for d in range(COLUMN - 1):
-            total = total + col_in[half, d]
+            total = total + col_in[half, d].astype(jnp.float32)
         stepped = before - total * rate
         blocks = []
         for b in range(3):
@@ -172,8 +191,7 @@
             blocks.append(new * (old_norm / new_norm))
         nw[half, core, plane] = jnp.concatenate(blocks, axis=1).astype(jnp.bfloat16)
 
-        @pl.loop(1, PLANE)
-        def _(d):
+        for d in FAR_FIRST:
             send(
                 nw.at[half, core, plane], nw.at[half, core, plane],
                 half_sems.at[half, 6], half_sems.at[half, 7], plane_peer(d),
@@ -196,38 +214,44 @@
 
     own_l, own_o = piece_out.at[0], piece_out.at[1]
 
-    away = grads(other, fw_ref[2 * mem + other].astype(jnp.bfloat16))
-    own_l[...] = grads(core, fw_ref[2 * mem + core].astype(jnp.bfloat16))
+    away = grads(other, fw_ref[other].astype(jnp.bfloat16))
+    own_l[...] = grads(core, fw_ref[core].astype(jnp.bfloat16))
 
     pl.semaphore_wait(barrier, PLANE - 1 + COLUMN - 1 + 4)
 
     first = pl.ds(pl.multiple_of(plane * PIECE, PIECE), PIECE)
     crossing = send(
-        fw_ref.at[2 * (1 - mem) + core, first], cross,
+        fw_hbm.at[2 * (1 - mem) + core, first], cross,
         sems.at[2], sems.at[3], tok, 1 - mem,
     )
     crossing.start()
     core_l = core_start(0, away)
 
+    blocks = rows // HD
     halos = []
-    middle = pl.ds(rows, rows)
-    for n, buf in enumerate((kx, vx)):
-        halos.append(send(buf.at[middle], buf.at[pl.ds(0, rows)], halo_sems.at[n, 0], halo_sems.at[n, 1], right))
-        halos.append(send(buf.at[middle], buf.at[pl.ds(2 * rows, rows)], halo_sems.at[n, 2], halo_sems.at[n, 3], left))
-    for copy in halos:
-        copy.start()
-
-    scatter_start(0, core_l, own_l)
-
-    crossing.wait_recv()
-    wo[core, plane] = cross[...].astype(jnp.bfloat16)
-
-    @pl.loop(1, PLANE)
-    def _(d):
-        send(
-            wo.at[core, plane], wo.at[core, plane], sems.at[4], sems.at[5], plane_peer(d)
-        ).start()
-
+    for n in range(2 * blocks):
+        buf = (kx, vx)[n % 2]
+        near, far = n // 2, blocks - 1 - n // 2
+        halos.append((
+            send(
+                buf.at[pl.ds(rows + far * HD, HD)], buf.at[pl.ds(far * HD, HD)],
+                halo_sems.at[n, 0], halo_sems.at[n, 1], right,
+            ),
+            send(
+                buf.at[pl.ds(rows + near * HD, HD)], buf.at[pl.ds(2 * rows + near * HD, HD)],
+                halo_sems.at[n, 2], halo_sems.at[n, 3], left,
+            ),
+        ))
+
+    def halo_start(n):
+        for copy in halos[n]:
+            copy.start()
+
+    halo_start(0)
+    halo_start(1)
+
+    for load in loads[4:]:
+        load.wait()
     count = len_ref.shape[1]
     lengths = len_ref[...].astype(jnp.float32)
     square = (count, count)
@@ -246,6 +270,82 @@
     query_views = jnp.sum(jnp.where(ends_row <= rows_f, 1.0, 0.0), axis=1, keepdims=True)
     qid[...] = jnp.broadcast_to(query_views, (rows, HD))
 
+    scatter_start(0, core_l, own_l)
+    halo_start(2)
+
+    factor = 1.0 / math.sqrt(HD) * math.log2(math.e)
+    heads = q_ref.shape[1] // HD
+
+    def attend_own(start, stop):
+        @pl.loop(start, stop)
+        def _(i):
+            here = pl.ds(pl.multiple_of(i * HD, HD), HD)
+            same = qid[here, :1] == kid[:, rows : 2 * rows]
+            for h in range(heads):
+                lanes = slice(h * HD, (h + 1) * HD)
+                scores = dot(q_ref[here, lanes], kx[middle, lanes], NT)
+                scores = jnp.where(same, scores * factor, -1e30)
+                peak = jnp.max(scores, axis=1, keepdims=True)
+                weight = jnp.exp2(scores - peak)
+                top[here, lanes] = jnp.broadcast_to(peak, (HD, HD))
+                mass[here, lanes] = jnp.broadcast_to(
+                    jnp.sum(weight, axis=1, keepdims=True), (HD, HD)
+                )
+                acc[here, lanes] = dot(weight.astype(jnp.bfloat16), vx[middle, lanes], NN)
+
+    def attend_more(start, stop, first_key):
+        keys = slice(first_key, first_key + HD)
+
+        @pl.loop(start, stop)
+        def _(i):
+            here = pl.ds(pl.multiple_of(i * HD, HD), HD)
+            same = qid[here, :] == kid[:, keys]
+            for h in range(heads):
+                lanes = slice(h * HD, (h + 1) * HD)
+                scores = dot(q_ref[here, lanes], kx[keys, lanes], NT)
+                scores = jnp.where(same, scores * factor, -1e30)
+                before = top[here, lanes]
+                peak = jnp.maximum(before, jnp.max(scores, axis=1, keepdims=True))
+                weight = jnp.exp2(scores - peak)
+                fade = jnp.exp2(before - peak)
+                top[here, lanes] = peak
+                mass[here, lanes] = mass[here, lanes] * fade + jnp.sum(
+                    weight, axis=1, keepdims=True
+                )
+                acc[here, lanes] = acc[here, lanes] * fade + dot(
+                    weight.astype(jnp.bfloat16), vx[keys, lanes], NN
+                )
+
+    def attend_halo(k):
+        for n in (2 * k, 2 * k + 1):
+            for copy in halos[n]:
+                copy.wait_recv()
+        attend_more(0, blocks - k, (blocks - 1 - k) * HD)
+        attend_more(k, blocks, 2 * rows + k * HD)
+
+    def read(half, j):
+        w = flat(nw[half, j]).astype(jnp.bfloat16)
+        qj = q_ref[:, j * DM : (j + 1) * DM]
+        pre = dot(qj, jnp.concatenate([w[:, :DM], w[:, DM : 2 * DM]], axis=0), NT)
+        gate, up = pre[:, :UNITS], pre[:, UNITS:]
+        hidden = (gate * jax.nn.sigmoid(gate) * up).astype(jnp.bfloat16)
+        return dot(hidden, w[:, 2 * DM :], NN)
+
+    attend_own(0, blocks // 2)
+
+    crossing.wait_recv()
+    wo[core, plane] = cross[...].astype(jnp.bfloat16)
+    for d in FAR_FIRST:
+        send(
+            wo.at[core, plane], wo.at[core, plane], sems.at[4], sems.at[5], plane_peer(d)
+        ).start()
+    halo_start(3)
+
+    attend_own(blocks // 2, blocks)
+
+    column_start(0, own_l)
+    halo_start(4)
+
     gathered = send(
         wo.at[core, pl.ds(0, PLANE - 1)], wo.at[core, pl.ds(0, PLANE - 1)],
         sems.at[4], sems.at[5], plane_peer(1),
@@ -253,53 +353,31 @@
     gathered.wait_recv()
     swapped = send(wo.at[core], wo.at[core], sems.at[6], sems.at[7], partner)
     swapped.start()
+    halo_start(5)
 
     own_o[...] = grads(core, flat(wo[core]).astype(jnp.bfloat16))
     swapped.wait_recv()
     core_o = core_start(1, grads(other, flat(wo[other]).astype(jnp.bfloat16)))
-
-    column_start(0, own_l)
+    halo_start(6)
+
+    update(0, fw_ref[core, first])
     scatter_start(1, core_o, own_o)
-    update(0, fw_ref[2 * mem + core, first])
+    halo_start(7)
+
+    attend_halo(0)
+    swap_l = swap_start(0)
+    attend_halo(1)
     column_start(1, own_o)
-    swap_l = swap_start(0)
+
+    swap_l.wait_recv()
+    for j in range(2):
+        told[:, j * DM : (j + 1) * DM] = read(0, j)
+
+    attend_halo(2)
     update(1, cross[...])
-
-    for copy in halos:
-        copy.wait_recv()
-
-    factor = 1.0 / math.sqrt(HD) * math.log2(math.e)
-    heads = q_ref.shape[1] // HD
-    reach = rows + rows + HD
-
-    @pl.loop(0, rows // HD)
-    def _(i):
-        here = pl.ds(pl.multiple_of(i * HD, HD), HD)
-        keys = pl.ds(pl.multiple_of(i * HD, HD), reach)
-        same = qid[here, :1] == kid[:, keys]
-        for h in range(heads):
-            lanes = slice(h * HD, (h + 1) * HD)
-            scores = dot(q_ref[here, lanes], kx[keys, lanes], NT)
-            scores = jnp.where(same, scores * factor, -1e30)
-            peak = jnp.max(scores, axis=1, keepdims=True)
-            weight = jnp.exp2(scores - peak)
-            mass = jnp.sum(weight, axis=1, keepdims=True)
-            acc[here, lanes] = dot(weight.astype(jnp.bfloat16), vx[keys, lanes], NN) / mass
-
-    swap_l.wait_recv()
+    attend_halo(3)
+    acc[...] = acc[...] / mass[...] + told[...]
     swap_o = swap_start(1)
-
-    def read(half, j):
-        w = flat(nw[half, j]).astype(jnp.bfloat16)
-        qj = q_ref[:, j * DM : (j + 1) * DM]
-        pre = dot(qj, jnp.concatenate([w[:, :DM], w[:, DM : 2 * DM]], axis=0), NT)
-        gate, up = pre[:, :UNITS], pre[:, UNITS:]
-        hidden = (gate * jax.nn.sigmoid(gate) * up).astype(jnp.bfloat16)
-        return dot(hidden, w[:, 2 * DM :], NN)
-
-    for j in range(2):
-        lanes = slice(j * DM, (j + 1) * DM)
-        acc[:, lanes] = acc[:, lanes] + read(0, j)
     swap_o.wait_recv()
     for j in range(2):
         lanes = slice(j * DM, (j + 1) * DM)
@@ -308,8 +386,9 @@
     crossing.wait_send()
     gathered.wait_send()
     swapped.wait_send()
-    for copy in halos:
-        copy.wait_send()
+    for pair in halos:
+        for copy in pair:
+            copy.wait_send()
     for half, (first_copy, last_copy) in enumerate(((core_l, swap_l), (core_o, swap_o))):
         first_copy.wait_send()
         whole(half).wait_send()
@@ -327,11 +406,18 @@
     return pl.pallas_call(
         body,
         out_shape=jax.ShapeDtypeStruct((rows, feats), bf),
-        in_specs=[vmem, hbm, hbm, vmem, vmem, vmem],
+        in_specs=[hbm] * 6,
         out_specs=vmem,
         scratch_shapes=[
+            pltpu.VMEM((rows, feats), bf),
+            pltpu.VMEM(step_sizes.shape, f32),
+            pltpu.VMEM((2,) + fast_weights.shape[1:], f32),
+            pltpu.VMEM((1,) + view_lengths.shape, jnp.int32),
             pltpu.VMEM((3 * rows, feats), bf),
             pltpu.VMEM((3 * rows, feats), bf),
+            pltpu.VMEM((rows, feats), f32),
+            pltpu.VMEM((rows, feats), f32),
+            pltpu.VMEM((rows, feats), f32),
             pltpu.VMEM((rows, feats), f32),
             pltpu.VMEM((1, 3 * rows), f32),
             pltpu.VMEM((rows, HD), f32),
@@ -341,15 +427,16 @@
             pltpu.VMEM((2,) + pieces, bf),
             pltpu.VMEM((2,) + pieces, f32),
             pltpu.VMEM((2, PLANE - 1, PIECE, WIDE), bf),
-            pltpu.VMEM((2, PIECE, WIDE), f32),
-            pltpu.VMEM((2, COLUMN - 1, PIECE, WIDE), f32),
+            pltpu.VMEM((2, PIECE, WIDE), bf),
+            pltpu.VMEM((2, COLUMN - 1, PIECE, WIDE), bf),
             pltpu.VMEM((2, 2) + pieces, bf),
             pltpu.SemaphoreType.DMA((8,)),
             pltpu.SemaphoreType.DMA((2, 10)),
-            pltpu.SemaphoreType.DMA((2, 4)),
+            pltpu.SemaphoreType.DMA((2 * (rows // HD), 4)),
+            pltpu.SemaphoreType.DMA((6,)),
         ],
         compiler_params=pltpu.CompilerParams(
-            collective_id=0, has_side_effects=True, vmem_limit_bytes=48 * 1024 * 1024
+            collective_id=0, has_side_effects=True, vmem_limit_bytes=VMEM_BYTES
         ),
     )(queries, keys, values, step_sizes, fast_weights, view_lengths.reshape(1, -1))
 

time: 60.5 us -> 59 us (0.975)
  local copies, waits for them, and re-layouts: 6.7 us -> 1.87 us
  Pallas kernels: 53.5 us -> 57 us
    unnamed x13 -> x1, local copies, waits for them, and re-layouts: 6.7 us -> 1.87 us
    pallas_call x1, Pallas kernels: 53.5 us -> 57 us  [on_device(): pl.pallas_call(body, out_shape=jax.ShapeDtypeStruct((rows, feats), bf), i...]
where the time goes in v2:
time: 59 us; the launch traced here: 58.9 us
  Pallas kernels  57 us (97%)
  local copies, waits for them, and re-layouts  1.87 us (3%)
    pallas_call x1, Pallas kernels, on_device(): pl.pallas_call(body, out_shape=jax.ShapeDtypeStruct((rows, feats), bf), i...  57 us
    unnamed x1, local copies, waits for them, and re-layouts  1.87 us

profile of v2, /device:TPU:1, one launch (start us, length us, event | category | flops | bytes accessed | tf_op | source)
XLA Modules:
  0.0 58.9 jit_solution(17144166708417090640)
XLA Ops:
  0.0 57.0 %shard_map.64 = bf16[512,512]{1,0:T(8,128)(2,1)} custom-call(bf16[512,512]{1,0:T(8,128)(2,1)} %q_hbm.1, bf16[512,512]{1,0:T(8,128)(2,1)} %k_hbm.1, bf16[512,512]{1,0:T(8,128)(2,1)} %v_hbm.1, f32[4,512]{1,0:T(4,128)} %step_hbm.1, f32[4,128,768]{2,1,0:T(8,128)} %fw_hbm.1, s32[1,256]{1,0:T(1,128)} %bitcast.1), custom_call_target="tpu_custom_call" | custom-call | tf_op jit(solution)/shard_map/pallas_call | solution.py:406
  57.0 1.9 %copy.8 = bf16[512,512]{1,0:T(8,128)(2,1)} copy(bf16[512,512]{1,0:T(8,128)(2,1)} %shard_map.64) | data formatting | bytes 1048576

commit v3 on v2

--- a/solution.py
+++ b/solution.py
@@ -14,7 +14,8 @@
 UNITS = 128
 PIECE = UNITS // PLANE
 WIDE = 3 * DM
-VMEM_BYTES = 66_000_000
+GROUP = 1
+VMEM_BYTES = 40 * 1024 * 1024
 MESH = pl.DeviceIdType.MESH
 SIDE = 4
 FAR_FIRST = sorted(
@@ -39,7 +40,7 @@
     q_hbm, k_hbm, v_hbm, step_hbm, fw_hbm, len_hbm, out_ref,
     q_ref, step_ref, fw_ref, len_ref, kx, vx, acc, top, mass, told, kid, qid,
     cross, wo, part, inbox, piece_out, piece_in, col_out, col_in, nw,
-    sems, half_sems, halo_sems, load_sems,
+    sems, half_sems, halo_sems, load_sems, hand_sems, plane_sems,
 ):
     tok = lax.axis_index("tok")
     mem = lax.axis_index("mem")
@@ -63,6 +64,10 @@
 
     def plane_peer(d):
         return plane_at(d) * 8 + spot
+
+    def plane_from(d):
+        across = lax.rem(plane // SIDE + SIDE - d // SIDE, SIDE)
+        return across * SIDE + lax.rem(lax.rem(plane, SIDE) + SIDE - d % SIDE, SIDE)
 
     def column_peer(d):
         return plane * 8 + lax.rem(level + d, COLUMN) * 2 + core
@@ -190,27 +195,38 @@
             new_norm = jnp.sqrt(jnp.sum(new * new, axis=1, keepdims=True) + norm_epsilon)
             blocks.append(new * (old_norm / new_norm))
         nw[half, core, plane] = jnp.concatenate(blocks, axis=1).astype(jnp.bfloat16)
-
+        gather_start(half)
+
+    def gathered_into(n):
+        return wo.at[core] if n == 2 else nw.at[n, core]
+
+    def plane_copy(n, piece, d):
+        buf = gathered_into(n)
+        return send(buf.at[piece], buf.at[piece], hand_sems.at[n, 0], plane_sems.at[n, d], plane_peer(d))
+
+    def hand_copy(n, piece):
+        buf = gathered_into(n)
+        return send(buf.at[piece], buf.at[piece], hand_sems.at[n, 1], hand_sems.at[n, 2], partner)
+
+    def hand_whole(n):
+        buf = gathered_into(n)
+        return send(buf, buf, hand_sems.at[n, 1], hand_sems.at[n, 2], partner)
+
+    def gather_start(n):
         for d in FAR_FIRST:
-            send(
-                nw.at[half, core, plane], nw.at[half, core, plane],
-                half_sems.at[half, 6], half_sems.at[half, 7], plane_peer(d),
-            ).start()
-
-    def gather_whole(half):
-        return send(
-            nw.at[half, core, pl.ds(0, PLANE - 1)], nw.at[half, core, pl.ds(0, PLANE - 1)],
-            half_sems.at[half, 6], half_sems.at[half, 7], plane_peer(1),
-        )
-
-    def swap_start(half):
-        gather_whole(half).wait_recv()
-        copy = send(
-            nw.at[half, core], nw.at[half, core],
-            half_sems.at[half, 8], half_sems.at[half, 9], partner,
-        )
-        copy.start()
-        return copy
+            plane_copy(n, plane, d).start()
+        hand_copy(n, plane).start()
+
+    def gather_pass(n):
+        for d in reversed(FAR_FIRST):
+            piece = plane_from(d)
+            plane_copy(n, piece, d).wait_recv()
+            hand_copy(n, piece).start()
+
+    def gather_sent(n):
+        buf = gathered_into(n).at[pl.ds(0, PLANE - 1)]
+        send(buf, buf, hand_sems.at[n, 0], plane_sems.at[n, 1], plane_peer(1)).wait_send()
+        hand_whole(n).wait_send()
 
     own_l, own_o = piece_out.at[0], piece_out.at[1]
 
@@ -247,8 +263,8 @@
         for copy in halos[n]:
             copy.start()
 
-    halo_start(0)
-    halo_start(1)
+    for n in range(3):
+        halo_start(n)
 
     for load in loads[4:]:
         load.wait()
@@ -271,61 +287,85 @@
     qid[...] = jnp.broadcast_to(query_views, (rows, HD))
 
     scatter_start(0, core_l, own_l)
-    halo_start(2)
 
     factor = 1.0 / math.sqrt(HD) * math.log2(math.e)
     heads = q_ref.shape[1] // HD
+
+    ones = jnp.ones((HD, HD), jnp.bfloat16)
+
+    def attend(here, spans, fresh):
+        views = qid[here, :]
+        same = [
+            jnp.concatenate([views] * (size // HD), axis=1) == kid[:, start : start + size]
+            for start, size in spans
+        ]
+        for head in range(0, heads, GROUP):
+            group = [slice(h * HD, (h + 1) * HD) for h in range(head, head + GROUP)]
+            scores = [
+                [
+                    jnp.where(
+                        mask, dot(q_ref[here, lanes], kx[start : start + size, lanes], NT) * factor, -1e30
+                    )
+                    for mask, (start, size) in zip(same, spans)
+                ]
+                for lanes in group
+            ]
+            peaks, fades, sums = [], [], []
+            for lanes, parts in zip(group, scores):
+                best = parts[0][:, :HD]
+                for part_scores in parts:
+                    for n in range(0, part_scores.shape[1], HD):
+                        best = jnp.maximum(best, part_scores[:, n : n + HD])
+                peak = jnp.broadcast_to(jnp.max(best, axis=1, keepdims=True), (HD, HD))
+                if not fresh:
+                    before = top[here, lanes]
+                    peak = jnp.maximum(peak, before)
+                    fades.append(jnp.exp2(before - peak))
+                peaks.append(peak)
+            for lanes, parts, peak in zip(group, scores, peaks):
+                total = None
+                for part_scores, (start, size) in zip(parts, spans):
+                    weight = jnp.exp2(
+                        part_scores - jnp.concatenate([peak] * (size // HD), axis=1)
+                    ).astype(jnp.bfloat16)
+                    beside = jnp.concatenate(
+                        [vx[start : start + size, lanes], jnp.concatenate([ones] * (size // HD), axis=0)],
+                        axis=1,
+                    )
+                    term = dot(weight, beside, NN)
+                    total = term if total is None else total + term
+                sums.append(total)
+            if not fresh:
+                sums = [
+                    total + fade_all * jnp.concatenate([acc[here, lanes], mass[here, lanes]], axis=1)
+                    for total, lanes, fade_all in zip(
+                        sums, group, [jnp.concatenate([fade, fade], axis=1) for fade in fades]
+                    )
+                ]
+            for lanes, peak, total in zip(group, peaks, sums):
+                top[here, lanes] = peak
+                acc[here, lanes] = total[:, :HD]
+                mass[here, lanes] = total[:, HD:]
 
     def attend_own(start, stop):
         @pl.loop(start, stop)
         def _(i):
-            here = pl.ds(pl.multiple_of(i * HD, HD), HD)
-            same = qid[here, :1] == kid[:, rows : 2 * rows]
-            for h in range(heads):
-                lanes = slice(h * HD, (h + 1) * HD)
-                scores = dot(q_ref[here, lanes], kx[middle, lanes], NT)
-                scores = jnp.where(same, scores * factor, -1e30)
-                peak = jnp.max(scores, axis=1, keepdims=True)
-                weight = jnp.exp2(scores - peak)
-                top[here, lanes] = jnp.broadcast_to(peak, (HD, HD))
-                mass[here, lanes] = jnp.broadcast_to(
-                    jnp.sum(weight, axis=1, keepdims=True), (HD, HD)
-                )
-                acc[here, lanes] = dot(weight.astype(jnp.bfloat16), vx[middle, lanes], NN)
-
-    def attend_more(start, stop, first_key):
-        keys = slice(first_key, first_key + HD)
-
-        @pl.loop(start, stop)
-        def _(i):
-            here = pl.ds(pl.multiple_of(i * HD, HD), HD)
-            same = qid[here, :] == kid[:, keys]
-            for h in range(heads):
-                lanes = slice(h * HD, (h + 1) * HD)
-                scores = dot(q_ref[here, lanes], kx[keys, lanes], NT)
-                scores = jnp.where(same, scores * factor, -1e30)
-                before = top[here, lanes]
-                peak = jnp.maximum(before, jnp.max(scores, axis=1, keepdims=True))
-                weight = jnp.exp2(scores - peak)
-                fade = jnp.exp2(before - peak)
-                top[here, lanes] = peak
-                mass[here, lanes] = mass[here, lanes] * fade + jnp.sum(
-                    weight, axis=1, keepdims=True
-                )
-                acc[here, lanes] = acc[here, lanes] * fade + dot(
-                    weight.astype(jnp.bfloat16), vx[keys, lanes], NN
-                )
-
-    def attend_halo(k):
-        for n in (2 * k, 2 * k + 1):
+            attend(pl.ds(pl.multiple_of(i * HD, HD), HD), [(rows, rows)], True)
+
+    def attend_halo(first_chunk, last_chunk):
+        for n in range(2 * first_chunk, 2 * last_chunk):
             for copy in halos[n]:
                 copy.wait_recv()
-        attend_more(0, blocks - k, (blocks - 1 - k) * HD)
-        attend_more(k, blocks, 2 * rows + k * HD)
+        for i in range(blocks):
+            low, high = max(i, blocks - last_chunk), blocks - first_chunk
+            spans = [(low * HD, (high - low) * HD)] if high > low else []
+            low, high = first_chunk, min(i + 1, last_chunk)
+            spans += [(2 * rows + low * HD, (high - low) * HD)] if high > low else []
+            attend(pl.ds(i * HD, HD), spans, False)
 
     def read(half, j):
         w = flat(nw[half, j]).astype(jnp.bfloat16)
-        qj = q_ref[:, j * DM : (j + 1) * DM]
+        qj = q_ref[:, pl.ds(pl.multiple_of(j * DM, DM), DM)]
         pre = dot(qj, jnp.concatenate([w[:, :DM], w[:, DM : 2 * DM]], axis=0), NT)
         gate, up = pre[:, :UNITS], pre[:, UNITS:]
         hidden = (gate * jax.nn.sigmoid(gate) * up).astype(jnp.bfloat16)
@@ -335,72 +375,62 @@
 
     crossing.wait_recv()
     wo[core, plane] = cross[...].astype(jnp.bfloat16)
-    for d in FAR_FIRST:
-        send(
-            wo.at[core, plane], wo.at[core, plane], sems.at[4], sems.at[5], plane_peer(d)
-        ).start()
+    gather_start(2)
+
+    attend_own(blocks // 2, blocks)
+
+    column_start(0, own_l)
     halo_start(3)
 
-    attend_own(blocks // 2, blocks)
-
-    column_start(0, own_l)
+    gather_pass(2)
     halo_start(4)
 
-    gathered = send(
-        wo.at[core, pl.ds(0, PLANE - 1)], wo.at[core, pl.ds(0, PLANE - 1)],
-        sems.at[4], sems.at[5], plane_peer(1),
-    )
-    gathered.wait_recv()
-    swapped = send(wo.at[core], wo.at[core], sems.at[6], sems.at[7], partner)
-    swapped.start()
+    own_o[...] = grads(core, flat(wo[core]).astype(jnp.bfloat16))
+    hand_whole(2).wait_recv()
+    core_o = core_start(1, grads(other, flat(wo[other]).astype(jnp.bfloat16)))
     halo_start(5)
-
-    own_o[...] = grads(core, flat(wo[core]).astype(jnp.bfloat16))
-    swapped.wait_recv()
-    core_o = core_start(1, grads(other, flat(wo[other]).astype(jnp.bfloat16)))
+    scatter_start(1, core_o, own_o)
     halo_start(6)
 
     update(0, fw_ref[core, first])
-    scatter_start(1, core_o, own_o)
+    attend_halo(0, 2)
+    column_start(1, own_o)
     halo_start(7)
-
-    attend_halo(0)
-    swap_l = swap_start(0)
-    attend_halo(1)
-    column_start(1, own_o)
-
-    swap_l.wait_recv()
+    gather_pass(0)
+
+    hand_whole(0).wait_recv()
     for j in range(2):
         told[:, j * DM : (j + 1) * DM] = read(0, j)
 
-    attend_halo(2)
     update(1, cross[...])
-    attend_halo(3)
+    attend_halo(2, 4)
     acc[...] = acc[...] / mass[...] + told[...]
-    swap_o = swap_start(1)
-    swap_o.wait_recv()
-    for j in range(2):
-        lanes = slice(j * DM, (j + 1) * DM)
+    gather_pass(1)
+
+    def finish(j):
+        lanes = pl.ds(pl.multiple_of(j * DM, DM), DM)
         out_ref[:, lanes] = (acc[:, lanes] + read(1, j)).astype(jnp.bfloat16)
 
+    finish(core)
+    hand_whole(1).wait_recv()
+    finish(other)
+
     crossing.wait_send()
-    gathered.wait_send()
-    swapped.wait_send()
     for pair in halos:
         for copy in pair:
             copy.wait_send()
-    for half, (first_copy, last_copy) in enumerate(((core_l, swap_l), (core_o, swap_o))):
+    for half, first_copy in enumerate((core_l, core_o)):
         first_copy.wait_send()
         whole(half).wait_send()
         column_whole(half).wait_send()
-        gather_whole(half).wait_send()
-        last_copy.wait_send()
+    for n in range(3):
+        gather_sent(n)
 
 
 def on_device(queries, keys, values, step_sizes, fast_weights, view_lengths):
     rows, feats = queries.shape
     vmem = pl.BlockSpec(memory_space=pltpu.VMEM)
-    hbm = pl.BlockSpec(memory_space=pl.ANY)
+    hbm = pl.BlockSpec(memory_space=pltpu.HBM)
     bf, f32 = jnp.bfloat16, jnp.float32
     pieces = (PLANE, PIECE, WIDE)
     return pl.pallas_call(
@@ -430,15 +460,17 @@
             pltpu.VMEM((2, PIECE, WIDE), bf),
             pltpu.VMEM((2, COLUMN - 1, PIECE, WIDE), bf),
             pltpu.VMEM((2, 2) + pieces, bf),
-            pltpu.SemaphoreType.DMA((8,)),
-            pltpu.SemaphoreType.DMA((2, 10)),
+            pltpu.SemaphoreType.DMA((4,)),
+            pltpu.SemaphoreType.DMA((2, 6)),
             pltpu.SemaphoreType.DMA((2 * (rows // HD), 4)),
             pltpu.SemaphoreType.DMA((6,)),
+            pltpu.SemaphoreType.DMA((3, 3)),
+            pltpu.SemaphoreType.DMA((3, PLANE)),
         ],
         compiler_params=pltpu.CompilerParams(
             collective_id=0, has_side_effects=True, vmem_limit_bytes=VMEM_BYTES
         ),
-    )(queries, keys, values, step_sizes, fast_weights, view_lengths.reshape(1, -1))
+    )(*[pltpu.with_memory_space_constraint(a, pltpu.HBM) for a in (queries, keys, values, step_sizes, fast_weights, view_lengths.reshape(1, -1))])
 
 
 def solution(mesh):

time: 59 us -> 47 us (0.80)
  Pallas kernels: 57 us -> 46.1 us
  local copies, waits for them, and re-layouts: 1.87 us -> 0.8 us
    pallas_call x1, Pallas kernels: 57 us -> 46.1 us  [on_device(): pl.pallas_call(body, out_shape=jax.ShapeDtypeStruct((rows, feats), bf), i...]
    unnamed x1, local copies, waits for them, and re-layouts: 1.87 us -> 0.8 us
where the time goes in v3:
time: 47 us; the launch traced here: 46.9 us
  Pallas kernels  46.1 us (98%)
  local copies, waits for them, and re-layouts  0.8 us (2%)
    pallas_call x1, Pallas kernels, on_device(): pl.pallas_call(body, out_shape=jax.ShapeDtypeStruct((rows, feats), bf), i...  46.1 us

profile of v3, /device:TPU:1, one launch (start us, length us, event | category | flops | bytes accessed | tf_op | source)
XLA Modules:
  0.0 46.9 jit_solution(10263690454031551703)
XLA Ops:
  0.0 46.1 %shard_map.64 = bf16[512,512]{1,0:T(8,128)(2,1)S(1)} custom-call(bf16[512,512]{1,0:T(8,128)(2,1)} %q_hbm.1, bf16[512,512]{1,0:T(8,128)(2,1)} %k_hbm.1, bf16[512,512]{1,0:T(8,128)(2,1)} %v_hbm.1, f32[4,512]{1,0:T(4,128)} %step_hbm.1, f32[4,128,768]{2,1,0:T(8,128)} %fw_hbm.1, s32[1,256]{1,0:T(1,128)} %bitcast.1), custom_call_target="tpu_custom_call" | custom-call | tf_op jit(solution)/shard_map/pallas_call | solution.py:436
  46.1 0.8 %copy.8 = bf16[512,512]{1,0:T(8,128)(2,1)} copy(bf16[512,512]{1,0:T(8,128)(2,1)S(1)} %shard_map.64) | data formatting | bytes 1048576

commit v4 on v3

--- a/solution.py
+++ b/solution.py
@@ -39,14 +39,15 @@
 def body(
     q_hbm, k_hbm, v_hbm, step_hbm, fw_hbm, len_hbm, out_ref,
     q_ref, step_ref, fw_ref, len_ref, kx, vx, acc, top, mass, told, kid, qid,
-    cross, wo, part, inbox, piece_out, piece_in, col_out, col_in, nw,
-    sems, half_sems, halo_sems, load_sems, hand_sems, plane_sems,
+    rows_out, rows_in, cast_out, cast_in, wo, part, inbox, piece_out, piece_in, col_out, col_in, nw,
+    half_sems, halo_sems, load_sems, swap_sems, cross_sems,
 ):
     tok = lax.axis_index("tok")
     mem = lax.axis_index("mem")
     n_tok = lax.axis_size("tok")
     rows = q_ref.shape[0]
     mine = pl.ds(2 * mem, 2)
+    first = pl.ds(pl.multiple_of(lax.axis_index("tok") // 8 * PIECE, PIECE), PIECE)
     core = lax.rem(tok, 2)
     other = 1 - core
     plane = tok // 8
@@ -65,12 +66,13 @@
     def plane_peer(d):
         return plane_at(d) * 8 + spot
 
-    def plane_from(d):
-        across = lax.rem(plane // SIDE + SIDE - d // SIDE, SIDE)
-        return across * SIDE + lax.rem(lax.rem(plane, SIDE) + SIDE - d % SIDE, SIDE)
-
     def column_peer(d):
         return plane * 8 + lax.rem(level + d, COLUMN) * 2 + core
+
+    def beyond(to_level):
+        return plane * 8 + to_level * 2 + core
+
+    edge = (level == 0) | (level == COLUMN - 1)
 
     def send(src, dst, s_sem, r_sem, tok_id, mem_id=None):
         return pltpu.make_async_remote_copy(
@@ -87,6 +89,7 @@
             (k_hbm, kx.at[middle]),
             (v_hbm, vx.at[middle]),
             (step_hbm, step_ref),
+            (fw_hbm.at[2 * (1 - mem) + core, first], rows_out),
             (len_hbm, len_ref),
             (q_hbm, q_ref),
         ))
@@ -102,7 +105,7 @@
         )
 
     greet(partner, mem)
-    greet(tok, 1 - mem)
+    greet(beyond(jnp.where(level < 2, COLUMN - 1, 0)), 1 - mem)
     greet(left, mem)
     greet(right, mem)
 
@@ -113,7 +116,7 @@
     def _(d):
         greet(column_peer(d), mem)
 
-    for load in loads[:4]:
+    for load in loads[:5]:
         load.wait()
 
     def grads(j, wb):
@@ -200,47 +203,46 @@
     def gathered_into(n):
         return wo.at[core] if n == 2 else nw.at[n, core]
 
-    def plane_copy(n, piece, d):
+    def gather_start(n):
         buf = gathered_into(n)
-        return send(buf.at[piece], buf.at[piece], hand_sems.at[n, 0], plane_sems.at[n, d], plane_peer(d))
-
-    def hand_copy(n, piece):
+        for d in FAR_FIRST:
+            send(
+                buf.at[plane], buf.at[plane], swap_sems.at[n, 0], swap_sems.at[n, 1], plane_peer(d)
+            ).start()
+
+    def gather_whole(n):
+        buf = gathered_into(n).at[pl.ds(0, PLANE - 1)]
+        return send(buf, buf, swap_sems.at[n, 0], swap_sems.at[n, 1], plane_peer(1))
+
+    def swap_whole(n):
         buf = gathered_into(n)
-        return send(buf.at[piece], buf.at[piece], hand_sems.at[n, 1], hand_sems.at[n, 2], partner)
-
-    def hand_whole(n):
-        buf = gathered_into(n)
-        return send(buf, buf, hand_sems.at[n, 1], hand_sems.at[n, 2], partner)
-
-    def gather_start(n):
-        for d in FAR_FIRST:
-            plane_copy(n, plane, d).start()
-        hand_copy(n, plane).start()
-
-    def gather_pass(n):
-        for d in reversed(FAR_FIRST):
-            piece = plane_from(d)
-            plane_copy(n, piece, d).wait_recv()
-            hand_copy(n, piece).start()
-
-    def gather_sent(n):
-        buf = gathered_into(n).at[pl.ds(0, PLANE - 1)]
-        send(buf, buf, hand_sems.at[n, 0], plane_sems.at[n, 1], plane_peer(1)).wait_send()
-        hand_whole(n).wait_send()
+        return send(buf, buf, swap_sems.at[n, 2], swap_sems.at[n, 3], partner)
+
+    def swap_start(n):
+        gather_whole(n).wait_recv()
+        swap_whole(n).start()
 
     own_l, own_o = piece_out.at[0], piece_out.at[1]
 
     away = grads(other, fw_ref[other].astype(jnp.bfloat16))
     own_l[...] = grads(core, fw_ref[core].astype(jnp.bfloat16))
 
-    pl.semaphore_wait(barrier, PLANE - 1 + COLUMN - 1 + 4)
-
-    first = pl.ds(pl.multiple_of(plane * PIECE, PIECE), PIECE)
-    crossing = send(
-        fw_hbm.at[2 * (1 - mem) + core, first], cross,
-        sems.at[2], sems.at[3], tok, 1 - mem,
-    )
-    crossing.start()
+    cast_out[...] = rows_out[...].astype(jnp.bfloat16)
+
+    pl.semaphore_wait(barrier, PLANE - 1 + COLUMN - 1 + 3 + jnp.where(edge, 2, 0))
+
+    def crossing(n, hop):
+        to_level = jnp.where(level == 0, COLUMN - 1 - hop, hop)
+        src, dst = ((cast_out, cast_in), (rows_out, rows_in))[n]
+        return send(
+            src, dst, cross_sems.at[n, hop], cross_sems.at[n, 2], beyond(to_level), 1 - mem
+        )
+
+    @pl.when(edge)
+    def _():
+        for hop in range(2):
+            crossing(0, hop).start()
+
     core_l = core_start(0, away)
 
     blocks = rows // HD
@@ -263,10 +265,10 @@
         for copy in halos[n]:
             copy.start()
 
-    for n in range(3):
+
+    for n in range(0, 1):
         halo_start(n)
-
-    for load in loads[4:]:
+    for load in loads[5:]:
         load.wait()
     count = len_ref.shape[1]
     lengths = len_ref[...].astype(jnp.float32)
@@ -287,6 +289,8 @@
     qid[...] = jnp.broadcast_to(query_views, (rows, HD))
 
     scatter_start(0, core_l, own_l)
+    for n in range(1, 3):
+        halo_start(n)
 
     factor = 1.0 / math.sqrt(HD) * math.log2(math.e)
     heads = q_ref.shape[1] // HD
@@ -361,61 +365,68 @@
             spans = [(low * HD, (high - low) * HD)] if high > low else []
             low, high = first_chunk, min(i + 1, last_chunk)
             spans += [(2 * rows + low * HD, (high - low) * HD)] if high > low else []
-            attend(pl.ds(i * HD, HD), spans, False)
+            if spans:
+                attend(pl.ds(i * HD, HD), spans, False)
+
+    def lanes_of(j):
+        return pl.ds(pl.multiple_of(j * DM, DM), DM)
 
     def read(half, j):
         w = flat(nw[half, j]).astype(jnp.bfloat16)
-        qj = q_ref[:, pl.ds(pl.multiple_of(j * DM, DM), DM)]
+        qj = q_ref[:, lanes_of(j)]
         pre = dot(qj, jnp.concatenate([w[:, :DM], w[:, DM : 2 * DM]], axis=0), NT)
         gate, up = pre[:, :UNITS], pre[:, UNITS:]
         hidden = (gate * jax.nn.sigmoid(gate) * up).astype(jnp.bfloat16)
         return dot(hidden, w[:, 2 * DM :], NN)
 
-    attend_own(0, blocks // 2)
-
-    crossing.wait_recv()
-    wo[core, plane] = cross[...].astype(jnp.bfloat16)
+    crossing(0, 0).wait_recv()
+    wo[core, plane] = cast_in[...]
     gather_start(2)
-
-    attend_own(blocks // 2, blocks)
+    for n in range(3, 7):
+        halo_start(n)
+
+    attend_own(0, blocks)
 
     column_start(0, own_l)
-    halo_start(3)
-
-    gather_pass(2)
-    halo_start(4)
-
+    for n in range(7, 8):
+        halo_start(n)
+
+    @pl.when(edge)
+    def _():
+        for hop in range(2):
+            crossing(1, hop).start()
+
+    swap_start(2)
     own_o[...] = grads(core, flat(wo[core]).astype(jnp.bfloat16))
-    hand_whole(2).wait_recv()
+    swap_whole(2).wait_recv()
     core_o = core_start(1, grads(other, flat(wo[other]).astype(jnp.bfloat16)))
-    halo_start(5)
     scatter_start(1, core_o, own_o)
-    halo_start(6)
-
+
+    attend_halo(0, 1)
+    column_start(1, own_o)
     update(0, fw_ref[core, first])
-    attend_halo(0, 2)
-    column_start(1, own_o)
-    halo_start(7)
-    gather_pass(0)
-
-    hand_whole(0).wait_recv()
-    for j in range(2):
-        told[:, j * DM : (j + 1) * DM] = read(0, j)
-
-    update(1, cross[...])
+    crossing(1, 0).wait_recv()
+    update(1, rows_in[...])
+    attend_halo(1, 2)
+
+    swap_start(0)
+    told[:, lanes_of(core)] = read(0, core)
+    swap_whole(0).wait_recv()
+    told[:, lanes_of(other)] = read(0, other)
+
+    swap_start(1)
     attend_halo(2, 4)
-    acc[...] = acc[...] / mass[...] + told[...]
-    gather_pass(1)
-
-    def finish(j):
-        lanes = pl.ds(pl.multiple_of(j * DM, DM), DM)
-        out_ref[:, lanes] = (acc[:, lanes] + read(1, j)).astype(jnp.bfloat16)
-
-    finish(core)
-    hand_whole(1).wait_recv()
-    finish(other)
-
-    crossing.wait_send()
+    told[:, lanes_of(core)] += read(1, core)
+    swap_whole(1).wait_recv()
+    told[:, lanes_of(other)] += read(1, other)
+    out_ref[...] = (acc[...] / mass[...] + told[...]).astype(jnp.bfloat16)
+
+    @pl.when(edge)
+    def _():
+        for n in range(2):
+            for hop in range(2):
+                crossing(n, hop).wait_send()
+
     for pair in halos:
         for copy in pair:
             copy.wait_send()
@@ -424,7 +435,8 @@
         whole(half).wait_send()
         column_whole(half).wait_send()
     for n in range(3):
-        gather_sent(n)
+        gather_whole(n).wait_send()
+        swap_whole(n).wait_send()
 
 
 def on_device(queries, keys, values, step_sizes, fast_weights, view_lengths):
@@ -452,6 +464,9 @@
             pltpu.VMEM((1, 3 * rows), f32),
             pltpu.VMEM((rows, HD), f32),
             pltpu.VMEM((PIECE, WIDE), f32),
+            pltpu.VMEM((PIECE, WIDE), f32),
+            pltpu.VMEM((PIECE, WIDE), bf),
+            pltpu.VMEM((PIECE, WIDE), bf),
             pltpu.VMEM((2,) + pieces, bf),
             pltpu.VMEM((2, 2) + pieces, bf),
             pltpu.VMEM((2,) + pieces, bf),
@@ -460,12 +475,11 @@
             pltpu.VMEM((2, PIECE, WIDE), bf),
             pltpu.VMEM((2, COLUMN - 1, PIECE, WIDE), bf),
             pltpu.VMEM((2, 2) + pieces, bf),
-            pltpu.SemaphoreType.DMA((4,)),
             pltpu.SemaphoreType.DMA((2, 6)),
             pltpu.SemaphoreType.DMA((2 * (rows // HD), 4)),
-            pltpu.SemaphoreType.DMA((6,)),
-            pltpu.SemaphoreType.DMA((3, 3)),
-            pltpu.SemaphoreType.DMA((3, PLANE)),
+            pltpu.SemaphoreType.DMA((7,)),
+            pltpu.SemaphoreType.DMA((3, 4)),
+            pltpu.SemaphoreType.DMA((2, 3)),
         ],
         compiler_params=pltpu.CompilerParams(
             collective_id=0, has_side_effects=True, vmem_limit_bytes=VMEM_BYTES

time: 47 us -> 45.5 us (0.968)
  Pallas kernels: 46.1 us -> 44.6 us
    pallas_call x1, Pallas kernels: 46.1 us -> 44.6 us  [on_device(): pl.pallas_call(body, out_shape=jax.ShapeDtypeStruct((rows, feats), bf), i...]
where the time goes in v4:
time: 45.5 us; the launch traced here: 45.4 us
  Pallas kernels  44.6 us (98%)
  local copies, waits for them, and re-layouts  0.8 us (2%)
    pallas_call x1, Pallas kernels, on_device(): pl.pallas_call(body, out_shape=jax.ShapeDtypeStruct((rows, feats), bf), i...  44.6 us

profile of v4, /device:TPU:1, one launch (start us, length us, event | category | flops | bytes accessed | tf_op | source)
XLA Modules:
  0.0 45.4 jit_solution(10542170169835421044)
XLA Ops:
  0.0 44.6 %shard_map.64 = bf16[512,512]{1,0:T(8,128)(2,1)S(1)} custom-call(bf16[512,512]{1,0:T(8,128)(2,1)} %q_hbm.1, bf16[512,512]{1,0:T(8,128)(2,1)} %k_hbm.1, bf16[512,512]{1,0:T(8,128)(2,1)} %v_hbm.1, f32[4,512]{1,0:T(4,128)} %step_hbm.1, f32[4,128,768]{2,1,0:T(8,128)} %fw_hbm.1, s32[1,256]{1,0:T(1,128)} %bitcast.1), custom_call_target="tpu_custom_call" | custom-call | tf_op jit(solution)/shard_map/pallas_call | solution.py:448
  44.6 0.8 %copy.8 = bf16[512,512]{1,0:T(8,128)(2,1)} copy(bf16[512,512]{1,0:T(8,128)(2,1)S(1)} %shard_map.64) | data formatting | bytes 1048576

commit v5 on v4

--- a/solution.py
+++ b/solution.py
@@ -243,7 +243,6 @@
         for hop in range(2):
             crossing(0, hop).start()
 
-    core_l = core_start(0, away)
 
     blocks = rows // HD
     halos = []
@@ -268,6 +267,8 @@
 
     for n in range(0, 1):
         halo_start(n)
+    core_l = core_start(0, away)
+
     for load in loads[5:]:
         load.wait()
     count = len_ref.shape[1]
@@ -382,14 +383,12 @@
     crossing(0, 0).wait_recv()
     wo[core, plane] = cast_in[...]
     gather_start(2)
-    for n in range(3, 7):
+    for n in range(3, 6):
         halo_start(n)
 
     attend_own(0, blocks)
 
     column_start(0, own_l)
-    for n in range(7, 8):
-        halo_start(n)
 
     @pl.when(edge)
     def _():
@@ -401,9 +400,13 @@
     swap_whole(2).wait_recv()
     core_o = core_start(1, grads(other, flat(wo[other]).astype(jnp.bfloat16)))
     scatter_start(1, core_o, own_o)
+    for n in range(6, 7):
+        halo_start(n)
 
     attend_halo(0, 1)
     column_start(1, own_o)
+    for n in range(7, 8):
+        halo_start(n)
     update(0, fw_ref[core, first])
     crossing(1, 0).wait_recv()
     update(1, rows_in[...])
@@ -415,10 +418,11 @@
     told[:, lanes_of(other)] = read(0, other)
 
     swap_start(1)
-    attend_halo(2, 4)
+    attend_halo(2, 3)
     told[:, lanes_of(core)] += read(1, core)
     swap_whole(1).wait_recv()
     told[:, lanes_of(other)] += read(1, other)
+    attend_halo(3, 4)
     out_ref[...] = (acc[...] / mass[...] + told[...]).astype(jnp.bfloat16)
 
     @pl.when(edge)

time: 45.5 us -> 44.5 us (0.978)
  Pallas kernels: 44.6 us -> 43.6 us
    pallas_call x1, Pallas kernels: 44.6 us -> 43.6 us  [on_device(): pl.pallas_call(body, out_shape=jax.ShapeDtypeStruct((rows, feats), bf), i...]
where the time goes in v5:
time: 44.5 us; the launch traced here: 44.4 us
  Pallas kernels  43.6 us (98%)
  local copies, waits for them, and re-layouts  0.8 us (2%)
    pallas_call x1, Pallas kernels, on_device(): pl.pallas_call(body, out_shape=jax.ShapeDtypeStruct((rows, feats), bf), i...  43.6 us

profile of v5, /device:TPU:1, one launch (start us, length us, event | category | flops | bytes accessed | tf_op | source)
XLA Modules:
  0.0 44.4 jit_solution(15688370952398427648)
XLA Ops:
  0.0 43.6 %shard_map.64 = bf16[512,512]{1,0:T(8,128)(2,1)S(1)} custom-call(bf16[512,512]{1,0:T(8,128)(2,1)} %q_hbm.1, bf16[512,512]{1,0:T(8,128)(2,1)} %k_hbm.1, bf16[512,512]{1,0:T(8,128)(2,1)} %v_hbm.1, f32[4,512]{1,0:T(4,128)} %step_hbm.1, f32[4,128,768]{2,1,0:T(8,128)} %fw_hbm.1, s32[1,256]{1,0:T(1,128)} %bitcast.1), custom_call_target="tpu_custom_call" | custom-call | tf_op jit(solution)/shard_map/pallas_call | solution.py:452
  43.6 0.8 %copy.8 = bf16[512,512]{1,0:T(8,128)(2,1)} copy(bf16[512,512]{1,0:T(8,128)(2,1)S(1)} %shard_map.64) | data formatting | bytes 1048576
